TPU v7x, 32 devices: a whole 2x2x4 slice. The times are simulated.
32 devices in a mesh: groups: 2 (over y), frame: 4 (over z), panel: 2 (over x), sub: 2 (over core).
Axes of the slice: x: 2, y: 2, z: 4, core: 2. Of those that a mesh axis runs over, the one named last changes fastest.
Arguments:
- frames: bfloat16 [2048, 65536], P(('groups', 'frame'), ('panel', 'sub')), parts along dimension 0, may hold values from -16 to 16
- slices: float32 [32, 65536], P(('groups', 'frame'), ('panel', 'sub')), parts along dimension 0, may hold values from -8 to 8
- log_prior: float32 [4096], replicated, may hold values from -2 to 2
- orient: int32 [32], P('groups'), parts along dimension 0, may hold values from 0 to 4095
Outputs:
- new_slices: float32 [32, 65536], P(('groups', 'frame'), ('panel', 'sub')), parts along dimension 0
There are 2 independent parts, one for each index of `groups`. A program takes and returns all parts, laid end to end along the dimension named above; an argument that names none is the same for every part. Nothing has to cross between parts.
All inputs are finite; a program needn't handle non-finite values.
Results may differ from a plain program's by a relative error of at most 0.022.
The roundings to bfloat16 on the way count: a program that leaves them out, or rounds other values in their place, can miss the bound.
Values may be sent and summed in bfloat16 or wider, within the bound.
A program may use at most 64 MiB of HBM per device.

v0:
```python
import math
import jax
import jax.numpy as jnp
from jax import lax
from jax.sharding import PartitionSpec as P

PIX = 65536
ITERS = 2


def fetch_slices(owned_b):
    return lax.all_gather(owned_b, "frame", axis=0, tiled=True)


def owner_update(weights, frames, counts, owned_b, offset):
    owned = owned_b.shape[0]
    mine = lax.psum_scatter(
        jnp.einsum("fm,fp->mp", weights, frames, preferred_element_type=jnp.float32).astype(
            jnp.bfloat16
        ),
        "frame",
        scatter_dimension=0,
        tiled=True,
    ).astype(jnp.float32)
    my_counts = lax.dynamic_slice_in_dim(counts, offset, owned, 0)
    return (mine + owned_b.astype(jnp.float32)) / (my_counts + 1.0)[:, None]


def local(frames, slices, log_prior, orient):
    owned = slices.shape[0]
    temper = 3.0 / math.sqrt(PIX)
    matches = orient[:, None] == jnp.arange(log_prior.shape[0], dtype=jnp.int32)[None, :]
    prior = jnp.sum(jnp.where(matches, log_prior[None, :], 0.0), axis=1)
    offset = lax.axis_index("frame") * owned
    current = slices
    owned_b = slices.astype(jnp.bfloat16)
    for step in range(ITERS):
        if step == 0:
            gathered = fetch_slices(owned_b)
        else:
            gathered = fetch_slices(owned_b)
        wide = gathered.astype(jnp.float32)
        norms = jnp.sum(wide * wide, axis=1)
        raw = (
            jnp.einsum("fp,mp->fm", frames, gathered, preferred_element_type=jnp.float32)
            - 0.5 * norms[None, :]
        )
        summed = lax.psum(raw, ("panel", "sub"))
        weights = jax.nn.softmax(temper * summed + prior[None, :], axis=1).astype(jnp.bfloat16)
        counts = lax.psum(jnp.sum(weights.astype(jnp.float32), axis=0), "frame")
        if step + 1 < ITERS:
            current = owner_update(weights, frames, counts, owned_b, offset)
            owned_b = current.astype(jnp.bfloat16)
        else:
            current = owner_update(weights, frames, counts, owned_b, offset)
    return current


def solution(mesh):
    in_specs = (
        P(("groups", "frame"), ("panel", "sub")),
        P(("groups", "frame"), ("panel", "sub")),
        P(),
        P("groups"),
    )
    out_specs = P(("groups", "frame"), ("panel", "sub"))
    return jax.shard_map(local, mesh=mesh, in_specs=in_specs, out_specs=out_specs, check_vma=False)
```

profile of v0, /device:TPU:0, one launch (start us, length us, event | category | flops | bytes accessed | tf_op | source)
XLA Modules:
  0.0 173.9 jit_solution(4613914813418080331)
XLA Ops:
  6.5 0.0 copy-start.2
  6.5 0.0 copy-start.1
  6.5 0.0 all-reduce.5.cloned.1.call-start
  6.5 1.0 convert_bitcast_fusion
  7.6 17.4 %all-gather = bf16[4,4,16384]{2,1,0:T(4,128)(2,1)S(1)} all-gather(bf16[1,4,16384]{2,1,0:T(4,128)(2,1)S(1)} %convert_bitcast_fusion), channel_id=1, replica_groups=mesh['groups'=2,'frame'=4,'panel'=2,'sub'=2] {'frame'}, dimensions={0}, use_global_device_ids=true | all-gather | bytes 655360 | tf_op jit(solution)/shard_map/all_gather | solution.py:12
  24.9 0.1 reshape.18
  25.1 0.2 multiply_reduce_fusion.1
  25.3 0.0 copy-start.3
  25.3 0.0 copy-start
  25.3 5.7 %convolution_subtract_fusion.1 = f32[256,16]{0,1:T(8,128)S(1)} fusion(bf16[256,16384]{1,0:T(8,128)(2,1)} %param.4, bf16[16,16384]{1,0:T(8,128)(2,1)S(1)} %reshape.18, f32[16]{0:T(128)S(1)} %broadcast_multiply_fusion.1), kind=kOutput, calls=%fused_computation.4 | convolution fusion | flops 134221824 | bytes 8929344 | tf_op jit(solution)/shard_map/fp,mp->fm/dot_general | solution.py:45
  31.0 10.1 %psum.28 = f32[256,16]{0,1:T(8,128)S(1)} all-reduce(f32[256,16]{0,1:T(8,128)S(1)} %convolution_subtract_fusion.1), channel_id=1, replica_groups=mesh['groups'=2,'frame'=4,'panel'=2,'sub'=2] {'panel','sub'}, use_global_device_ids=true, to_apply=%region_1.2 | all-reduce | flops 4096 | bytes 32768 | tf_op jit(solution)/shard_map/psum | solution.py:48
  41.1 0.0 copy-done.2
  41.1 0.0 copy-done.1
  41.1 0.2 select_reduce_fusion
  41.4 0.1 fusion.2
  41.5 0.1 fusion.4
  41.6 0.2 convert_reduce_fusion.1
  41.7 5.4 %convolution_convert_fusion.1 = bf16[16,16384]{1,0:T(8,128)(2,1)} fusion(bf16[256,16]{0,1:T(8,128)(2,1)S(1)} %get-tuple-element.8, bf16[256,16384]{1,0:T(8,128)(2,1)} %param.4), kind=kOutput, calls=%fused_computation.1 | convolution fusion | flops 134479872 | bytes 8921088 | tf_op jit(solution)/shard_map/fm,fp->mp/dot_general | solution.py:18
  47.2 0.0 all-reduce.5.cloned.1.call-update
  47.2 0.0 all-reduce.7.cloned.1.call-start
  47.2 0.0 copy-done.3
  47.3 0.6 dynamic-slice
  48.5 12.6 %psum.29 = f32[16]{0:T(128)S(1)} all-reduce(f32[16]{0:T(128)S(1)} %get-tuple-element.7), channel_id=1, replica_groups=mesh['groups'=2,'frame'=4,'panel'=2,'sub'=2] {'frame'}, use_global_device_ids=true, to_apply=%region_7.8 | all-reduce | flops 16 | bytes 128 | tf_op jit(solution)/shard_map/psum | solution.py:50
  61.0 0.1 dynamic-slice_add_fusion.1
  61.1 26.4 %all-reduce.5.cloned.1.call-done = bf16[16,16384]{1,0:T(8,128)(2,1)} async-done(((bf16[16,16384]{1,0:T(8,128)(2,1)}), bf16[16,16384]{1,0:T(8,128)(2,1)}) %all-reduce.5.cloned.1.call-update) | async-done | bytes 524304
  87.6 0.0 copy-done
  87.6 1.1 fusion.1
  88.6 16.2 %all-gather.1 = bf16[4,4,16384]{2,1,0:T(4,128)(2,1)S(1)} all-gather(bf16[1,4,16384]{2,1,0:T(4,128)(2,1)S(1)} %bitcast.14), channel_id=1, replica_groups=mesh['groups'=2,'frame'=4,'panel'=2,'sub'=2] {'frame'}, dimensions={0}, use_global_device_ids=true | all-gather | bytes 655360 | tf_op jit(solution)/shard_map/all_gather | solution.py:12
  104.8 0.1 reshape.20
  104.9 0.2 multiply_reduce_fusion
  105.2 5.6 %fusion = f32[256,16]{0,1:T(8,128)S(1)} fusion(bf16[16,16384]{1,0:T(8,128)(2,1)S(1)} %reshape.20, bf16[256,16384]{1,0:T(8,128)(2,1)} %param.4, f32[16]{0:T(128)S(1)} %broadcast_multiply_fusion), kind=kOutput, calls=%fused_computation.3 | convolution fusion | flops 134221824 | bytes 8929344 | tf_op jit(solution)/shard_map/fp,mp->fm/dot_general | solution.py:45
  110.8 10.1 %psum.30 = f32[256,16]{0,1:T(8,128)S(1)} all-reduce(f32[256,16]{0,1:T(8,128)S(1)} %fusion), channel_id=1, replica_groups=mesh['groups'=2,'frame'=4,'panel'=2,'sub'=2] {'panel','sub'}, use_global_device_ids=true, to_apply=%region_9.10 | all-reduce | flops 4096 | bytes 32768 | tf_op jit(solution)/shard_map/psum | solution.py:48
  120.9 0.1 fusion.3
  121.0 0.1 fusion.5
  121.1 0.2 convert_reduce_fusion
  121.3 5.4 %convolution_convert_fusion = bf16[16,16384]{1,0:T(8,128)(2,1)} fusion(bf16[256,16]{0,1:T(8,128)(2,1)S(1)} %get-tuple-element.6, bf16[256,16384]{1,0:T(8,128)(2,1)} %param.4), kind=kOutput, calls=%fused_computation | convolution fusion | flops 134479872 | bytes 8921088 | tf_op jit(solution)/shard_map/fm,fp->mp/dot_general | solution.py:18
  126.7 0.0 all-reduce.7.cloned.1.call-update
  126.7 10.8 %psum.31 = f32[16]{0:T(128)S(1)} all-reduce(f32[16]{0:T(128)S(1)} %get-tuple-element.5), channel_id=1, replica_groups=mesh['groups'=2,'frame'=4,'panel'=2,'sub'=2] {'frame'}, use_global_device_ids=true, to_apply=%region_14.15 | all-reduce | flops 16 | bytes 128 | tf_op jit(solution)/shard_map/psum | solution.py:50
  137.5 0.1 dynamic-slice_add_fusion
  137.6 27.7 %all-reduce.7.cloned.1.call-done = bf16[16,16384]{1,0:T(8,128)(2,1)} async-done(((bf16[16,16384]{1,0:T(8,128)(2,1)}), bf16[16,16384]{1,0:T(8,128)(2,1)}) %all-reduce.7.cloned.1.call-update) | async-done | bytes 524304
  165.3 1.8 %add_divide_fusion = f32[4,16384]{1,0:T(4,128)} fusion(bf16[4,16384]{1,0:T(4,128)(2,1)S(1)} %fusion.1, bf16[16,16384]{1,0:T(8,128)(2,1)} %all-reduce.7.cloned.1.call-done, u32[]{:T(128)S(6)} %multiply.1, f32[4]{0:T(128)S(1)} %dynamic-slice_add_fusion), kind=kLoop, calls=%fused_computation.7 | loop fusion | flops 262144 | bytes 524308 | tf_op jit(solution)/shard_map/div | solution.py:26
  (2 shorter events, 0.0 us)
Async XLA Ops:
  6.5 34.6 %copy-start.2 = (s32[16]{0:T(128)S(1)}, s32[16]{0:T(128)}, u32[]{:S(2)}) copy-start(s32[16]{0:T(128)} %param.7) | copy-start | bytes 196
  6.5 34.6 %copy-start.1 = (f32[4096]{0:T(1024)S(1)}, f32[4096]{0:T(1024)}, u32[]{:S(2)}) copy-start(f32[4096]{0:T(1024)} %param.6) | copy-start | bytes 49156
  6.5 81.0 %all-reduce.5.cloned.1.call-start = ((), (), s32[]{:S(2)}) async-start(), calls=%async_computation | async-start | bytes 1048576
  25.3 21.9 %copy-start.3 = (u32[32]{0:T(128)S(1)}, u32[32]{0:T(128)}, u32[]{:S(2)}) copy-start(u32[32]{0:T(128)} %constant.25) | copy-start | bytes 388
  25.3 62.2 %copy-start = (f32[4,16384]{1,0:T(4,128)S(1)}, f32[4,16384]{1,0:T(4,128)}, u32[]{:S(2)}) copy-start(f32[4,16384]{1,0:T(4,128)} %param.5) | copy-start | bytes 786436
  47.2 118.2 %all-reduce.7.cloned.1.call-start = ((), (), s32[]{:S(2)}) async-start(), calls=%async_computation.1 | async-start | bytes 1048576
Sparse Core Ops, SparseCore 0:
  47.3 40.1 all-reduce.4
  126.9 38.4 all-reduce.6
where the time goes:
time: 174 us
  blocking collectives  77.1 us (44%)
  waiting for transfers between devices  54.2 us (31%)
  matrix products  22.2 us (13%)
  between operations  14.1 us (8%)
  other arithmetic  5.48 us (3%)
    unnamed x4, waiting for transfers between devices  54.2 us
    all_gather x2, blocking collectives, fetch_slices(): return lax.all_gather(owned_b, 'frame', axis=0, tiled=True)  33.5 us
    psum x2, blocking collectives, local(): counts = lax.psum(jnp.sum(weights.astype(jnp.float32), axis=0), 'frame')  23.3 us
    psum x2, blocking collectives, local(): summed = lax.psum(raw, ('panel', 'sub'))  20.2 us
    dot_general x2, matrix products, local(): jnp.einsum('fp,mp->fm', frames, gathered, preferred_element_type=jnp.floa...  11.3 us
    dot_general x2, matrix products, owner_update(): jnp.einsum('fm,fp->mp', weights, frames, preferred_element_type=jnp.float32)  10.8 us
  transfers between devices with their start and end apart: 2, of which 2 were waited for; matrix products, arithmetic and copies ran while one was open for 0% of the time, Pallas kernels for 0%

commit v1 on v0

--- a/solution.py
+++ b/solution.py
@@ -8,8 +8,24 @@
 ITERS = 2
 
 
+def gather_around(x, axis, dim):
+    ways, here, turn = (lax.axis_size(axis), lax.axis_index(axis), x.shape[dim])
+    dims = [n * ways if d == dim else n for d, n in enumerate(x.shape)]
+    full = lax.dynamic_update_slice_in_dim(jnp.zeros(dims, x.dtype), x, here * turn, axis=dim)
+    going_up = going_down = x
+    for far in range(1, ways // 2 + 1):
+        going_up = lax.ppermute(going_up, axis, [(d, (d + 1) % ways) for d in range(ways)])
+        full = lax.dynamic_update_slice_in_dim(full, going_up, (here - far) % ways * turn, axis=dim)
+        if 2 * far < ways:
+            going_down = lax.ppermute(going_down, axis, [(d, (d - 1) % ways) for d in range(ways)])
+            full = lax.dynamic_update_slice_in_dim(
+                full, going_down, (here + far) % ways * turn, axis=dim
+            )
+    return full
+
+
 def fetch_slices(owned_b):
-    return lax.all_gather(owned_b, "frame", axis=0, tiled=True)
+    return gather_around(owned_b, "frame", 0)
 
 
 def owner_update(weights, frames, counts, owned_b, offset):

time: 174 us -> 167 us (0.960)
  blocking collectives: 77.1 us -> 39.6 us
  waiting for transfers between devices: 54.2 us -> 74 us
  starting transfers between devices: 0.04 us -> 9.57 us
    all_gather x2 -> x0, blocking collectives: 33.5 us -> none  [fetch_slices(): return lax.all_gather(owned_b, 'frame', axis=0, tiled=True)]
    ppermute x0 -> x6, waiting for transfers between devices: none -> 19.8 us  [the longest x4 18.5 us: gather_around(): lax.ppermute(going_up, axis, [(d, (d + 1) % ways) for d in range(ways)])]
    ppermute x0 -> x6, starting transfers between devices: none -> 9.53 us  [the longest x4 4.88 us: gather_around(): lax.ppermute(going_up, axis, [(d, (d + 1) % ways) for d in range(ways)])]
    psum x2, blocking collectives: 23.3 us -> 19.3 us  [local(): counts = lax.psum(jnp.sum(weights.astype(jnp.float32), axis=0), 'frame')]
    dynamic_update_slice x0 -> x2, other arithmetic: none -> 2.23 us  [gather_around(): lax.dynamic_update_slice_in_dim(jnp.zeros(dims, x.dtype), x, here * turn,...]
  transfers between devices with their start and end apart: 2 -> 8, of which waited for: 2 -> 7; matrix products, arithmetic and copies ran while one was open for 0% -> 1% of each run, Pallas kernels for 0% -> 0%
where the time goes in v1:
time: 167 us
  waiting for transfers between devices  74 us (44%)
  blocking collectives  39.6 us (24%)
  matrix products  22.1 us (13%)
  between operations  14.1 us (8%)
  starting transfers between devices  9.57 us (6%)
  other arithmetic  6.33 us (4%)
    unnamed x4, waiting for transfers between devices  54.2 us
    psum x2, blocking collectives, local(): summed = lax.psum(raw, ('panel', 'sub'))  20.2 us
    psum x2, blocking collectives, local(): counts = lax.psum(jnp.sum(weights.astype(jnp.float32), axis=0), 'frame')  19.3 us
    ppermute x4, waiting for transfers between devices, gather_around(): lax.ppermute(going_up, axis, [(d, (d + 1) % ways) for d in range(ways)])  18.5 us
    dot_general x2, matrix products, local(): jnp.einsum('fp,mp->fm', frames, gathered, preferred_element_type=jnp.floa...  11.3 us
    dot_general x2, matrix products, owner_update(): jnp.einsum('fm,fp->mp', weights, frames, preferred_element_type=jnp.float32)  10.8 us
    ppermute x4, starting transfers between devices, gather_around(): lax.ppermute(going_up, axis, [(d, (d + 1) % ways) for d in range(ways)])  4.88 us
    ppermute x2, starting transfers between devices, gather_around(): lax.ppermute(going_down, axis, [(d, (d - 1) % ways) for d in range(ways)])  4.65 us
  transfers between devices with their start and end apart: 8, of which 7 were waited for; matrix products, arithmetic and copies ran while one was open for 1% of the time, Pallas kernels for 0%

profile of v1, /device:TPU:0, one launch (start us, length us, event | category | flops | bytes accessed | tf_op | source)
XLA Modules:
  0.0 166.9 jit_solution(11557339152969574369)
XLA Ops:
  6.5 0.0 all-reduce.5.cloned.1.call-start
  6.6 1.1 constant_dynamic-update-slice_fusion.7
  7.7 3.1 %collective-permute-start = (bf16[4,16384]{1,0:T(4,128)(2,1)S(1)}, bf16[4,16384]{1,0:T(4,128)(2,1)S(1)}, u32[]{:S(2)}, u32[]{:S(2)}) collective-permute-start(bf16[4,16384]{1,0:T(4,128)(2,1)S(1)} %get-tuple-element.12), channel_id=1, source_target_pairs={{0,4},{4,8},{8,12},{12,0},{1,5},{5,9},{9,13},{13,1},{2,6},{6,10},{... | collective-permute-start | bytes 393224 | tf_op jit(solution)/shard_map/ppermute | solution.py:17
  10.7 2.1 %collective-permute-start.1 = (bf16[4,16384]{1,0:T(4,128)(2,1)S(1)}, bf16[4,16384]{1,0:T(4,128)(2,1)S(1)}, u32[]{:S(2)}, u32[]{:S(2)}) collective-permute-start(bf16[4,16384]{1,0:T(4,128)(2,1)S(1)} %get-tuple-element.12), channel_id=1, source_target_pairs={{0,12},{4,0},{8,4},{12,8},{1,13},{5,1},{9,5},{13,9},{2,14},{6,2},{... | collective-permute-start | bytes 393224 | tf_op jit(solution)/shard_map/ppermute | solution.py:20
  12.8 0.9 select_reduce_fusion
  13.8 3.3 %collective-permute-done = bf16[4,16384]{1,0:T(4,128)(2,1)S(1)} collective-permute-done((bf16[4,16384]{1,0:T(4,128)(2,1)S(1)}, bf16[4,16384]{1,0:T(4,128)(2,1)S(1)}, u32[]{:S(2)}, u32[]{:S(2)}) %collective-permute-start) | collective-permute-done | bytes 131104 | tf_op jit(solution)/shard_map/ppermute | solution.py:17
  17.1 0.0 collective-permute-start.2
  17.1 0.1 constant_dynamic-update-slice_fusion.6
  17.2 1.3 collective-permute-done.1
  18.5 0.1 constant_dynamic-update-slice_fusion.5
  18.6 5.3 %collective-permute-done.2 = bf16[4,16384]{1,0:T(4,128)(2,1)S(1)} collective-permute-done((bf16[4,16384]{1,0:T(4,128)(2,1)S(1)}, bf16[4,16384]{1,0:T(4,128)(2,1)S(1)}, u32[]{:S(2)}, u32[]{:S(2)}) %collective-permute-start.2) | collective-permute-done | bytes 131104 | tf_op jit(solution)/shard_map/ppermute | solution.py:17
  23.9 0.1 constant_dynamic-update-slice_fusion.4
  23.9 0.2 multiply_reduce_fusion.1
  24.2 0.0 copy-start
  24.2 5.6 %fusion.1 = f32[256,16]{0,1:T(8,128)S(1)} fusion(bf16[16,16384]{1,0:T(8,128)(2,1)S(1)} %constant_dynamic-update-slice_fusion.4, bf16[256,16384]{1,0:T(8,128)(2,1)} %param.4, f32[16]{0:T(128)S(1)} %broadcast_multiply_fusion.1), kind=kOutput, calls=%fused_computation.5 | convolution fusion | flops 134221824 | bytes 8929344 | tf_op jit(solution)/shard_map/fp,mp->fm/dot_general | solution.py:61
  29.9 10.1 %psum.28 = f32[256,16]{0,1:T(8,128)S(1)} all-reduce(f32[256,16]{0,1:T(8,128)S(1)} %fusion.1), channel_id=1, replica_groups=mesh['groups'=2,'frame'=4,'panel'=2,'sub'=2] {'panel','sub'}, use_global_device_ids=true, to_apply=%region_1.2 | all-reduce | flops 4096 | bytes 32768 | tf_op jit(solution)/shard_map/psum | solution.py:64
  40.0 0.1 fusion.3
  40.1 0.1 fusion.5
  40.2 0.2 convert_reduce_fusion.1
  40.4 5.4 %convolution_convert_fusion.1 = bf16[16,16384]{1,0:T(8,128)(2,1)} fusion(bf16[256,16]{0,1:T(8,128)(2,1)S(1)} %get-tuple-element.10, bf16[256,16384]{1,0:T(8,128)(2,1)} %param.4), kind=kOutput, calls=%fused_computation.1 | convolution fusion | flops 134479872 | bytes 8921088 | tf_op jit(solution)/shard_map/fm,fp->mp/dot_general | solution.py:34
  45.8 0.0 all-reduce.5.cloned.1.call-update
  45.8 0.0 all-reduce.7.cloned.1.call-start
  45.9 0.6 dynamic-slice
  47.1 10.4 %psum.29 = f32[16]{0:T(128)S(1)} all-reduce(f32[16]{0:T(128)S(1)} %get-tuple-element.9), channel_id=1, replica_groups=mesh['groups'=2,'frame'=4,'panel'=2,'sub'=2] {'frame'}, use_global_device_ids=true, to_apply=%region_7.8 | all-reduce | flops 16 | bytes 128 | tf_op jit(solution)/shard_map/psum | solution.py:66
  57.5 0.1 dynamic-slice_add_fusion.1
  57.6 26.2 %all-reduce.5.cloned.1.call-done = bf16[16,16384]{1,0:T(8,128)(2,1)} async-done(((bf16[16,16384]{1,0:T(8,128)(2,1)}), bf16[16,16384]{1,0:T(8,128)(2,1)}) %all-reduce.5.cloned.1.call-update) | async-done | bytes 524304
  83.8 1.2 constant_dynamic-update-slice_fusion.3
  85.0 1.3 collective-permute-start.3
  86.3 2.6 %collective-permute-start.4 = (bf16[4,16384]{1,0:T(4,128)(2,1)S(1)}, bf16[4,16384]{1,0:T(4,128)(2,1)S(1)}, u32[]{:S(2)}, u32[]{:S(2)}) collective-permute-start(bf16[4,16384]{1,0:T(4,128)(2,1)S(1)} %get-tuple-element.8), channel_id=1, source_target_pairs={{0,12},{4,0},{8,4},{12,8},{1,13},{5,1},{9,5},{13,9},{2,14},{6,2},{... | collective-permute-start | bytes 393224 | tf_op jit(solution)/shard_map/ppermute | solution.py:20
  88.8 3.8 %collective-permute-done.3 = bf16[4,16384]{1,0:T(4,128)(2,1)S(1)} collective-permute-done((bf16[4,16384]{1,0:T(4,128)(2,1)S(1)}, bf16[4,16384]{1,0:T(4,128)(2,1)S(1)}, u32[]{:S(2)}, u32[]{:S(2)}) %collective-permute-start.3) | collective-permute-done | bytes 131104 | tf_op jit(solution)/shard_map/ppermute | solution.py:17
  92.7 0.5 collective-permute-start.5
  93.2 0.1 constant_dynamic-update-slice_fusion.2
  93.3 0.0 collective-permute-done.4
  93.3 0.1 constant_dynamic-update-slice_fusion.1
  93.4 6.1 %collective-permute-done.5 = bf16[4,16384]{1,0:T(4,128)(2,1)S(1)} collective-permute-done((bf16[4,16384]{1,0:T(4,128)(2,1)S(1)}, bf16[4,16384]{1,0:T(4,128)(2,1)S(1)}, u32[]{:S(2)}, u32[]{:S(2)}) %collective-permute-start.5) | collective-permute-done | bytes 131104 | tf_op jit(solution)/shard_map/ppermute | solution.py:17
  99.5 0.1 constant_dynamic-update-slice_fusion
  99.5 0.2 multiply_reduce_fusion
  99.8 5.6 %fusion = f32[256,16]{0,1:T(8,128)S(1)} fusion(bf16[16,16384]{1,0:T(8,128)(2,1)S(1)} %constant_dynamic-update-slice_fusion, bf16[256,16384]{1,0:T(8,128)(2,1)} %param.4, f32[16]{0:T(128)S(1)} %broadcast_multiply_fusion), kind=kOutput, calls=%fused_computation.3 | convolution fusion | flops 134221824 | bytes 8929344 | tf_op jit(solution)/shard_map/fp,mp->fm/dot_general | solution.py:61
  105.4 10.1 %psum.30 = f32[256,16]{0,1:T(8,128)S(1)} all-reduce(f32[256,16]{0,1:T(8,128)S(1)} %fusion), channel_id=1, replica_groups=mesh['groups'=2,'frame'=4,'panel'=2,'sub'=2] {'panel','sub'}, use_global_device_ids=true, to_apply=%region_9.10 | all-reduce | flops 4096 | bytes 32768 | tf_op jit(solution)/shard_map/psum | solution.py:64
  115.6 0.1 fusion.4
  115.7 0.1 fusion.6
  115.8 0.2 convert_reduce_fusion
  115.9 5.4 %convolution_convert_fusion = bf16[16,16384]{1,0:T(8,128)(2,1)} fusion(bf16[256,16]{0,1:T(8,128)(2,1)S(1)} %get-tuple-element.6, bf16[256,16384]{1,0:T(8,128)(2,1)} %param.4), kind=kOutput, calls=%fused_computation | convolution fusion | flops 134479872 | bytes 8921088 | tf_op jit(solution)/shard_map/fm,fp->mp/dot_general | solution.py:34
  121.4 0.0 all-reduce.7.cloned.1.call-update
  121.4 8.9 %psum.31 = f32[16]{0:T(128)S(1)} all-reduce(f32[16]{0:T(128)S(1)} %get-tuple-element.5), channel_id=1, replica_groups=mesh['groups'=2,'frame'=4,'panel'=2,'sub'=2] {'frame'}, use_global_device_ids=true, to_apply=%region_14.15 | all-reduce | flops 16 | bytes 128 | tf_op jit(solution)/shard_map/psum | solution.py:66
  130.3 0.1 dynamic-slice_add_fusion
  130.4 27.9 %all-reduce.7.cloned.1.call-done = bf16[16,16384]{1,0:T(8,128)(2,1)} async-done(((bf16[16,16384]{1,0:T(8,128)(2,1)}), bf16[16,16384]{1,0:T(8,128)(2,1)}) %all-reduce.7.cloned.1.call-update) | async-done | bytes 524304
  158.3 1.8 %add_divide_fusion = f32[4,16384]{1,0:T(4,128)} fusion(bf16[4,16384]{1,0:T(4,128)(2,1)S(1)} %get-tuple-element.8, bf16[16,16384]{1,0:T(8,128)(2,1)} %all-reduce.7.cloned.1.call-done, u32[]{:T(128)S(6)} %multiply.1, f32[4]{0:T(128)S(1)} %dynamic-slice_add_fusion), kind=kLoop, calls=%fused_computation.8 | loop fusion | flops 262144 | bytes 524308 | tf_op jit(solution)/shard_map/div | solution.py:42
  (5 shorter events, 0.1 us)
Async XLA Ops:
  6.5 77.2 %all-reduce.5.cloned.1.call-start = ((), (), s32[]{:S(2)}) async-start(), calls=%async_computation | async-start | bytes 1048576
  7.7 9.4 %collective-permute-start = (bf16[4,16384]{1,0:T(4,128)(2,1)S(1)}, bf16[4,16384]{1,0:T(4,128)(2,1)S(1)}, u32[]{:S(2)}, u32[]{:S(2)}) collective-permute-start(bf16[4,16384]{1,0:T(4,128)(2,1)S(1)} %get-tuple-element.12), channel_id=1, source_target_pairs={{0,4},{4,8},{8,12},{12,0},{1,5},{5,9},{9,13},{13,1},{2,6},{6,10},{... | collective-permute-start | bytes 393224 | tf_op jit(solution)/shard_map/ppermute | solution.py:17
  10.7 7.8 %collective-permute-start.1 = (bf16[4,16384]{1,0:T(4,128)(2,1)S(1)}, bf16[4,16384]{1,0:T(4,128)(2,1)S(1)}, u32[]{:S(2)}, u32[]{:S(2)}) collective-permute-start(bf16[4,16384]{1,0:T(4,128)(2,1)S(1)} %get-tuple-element.12), channel_id=1, source_target_pairs={{0,12},{4,0},{8,4},{12,8},{1,13},{5,1},{9,5},{13,9},{2,14},{6,2},{... | collective-permute-start | bytes 393224 | tf_op jit(solution)/shard_map/ppermute | solution.py:20
  17.1 6.8 %collective-permute-start.2 = (bf16[4,16384]{1,0:T(4,128)(2,1)S(1)}, bf16[4,16384]{1,0:T(4,128)(2,1)S(1)}, u32[]{:S(2)}, u32[]{:S(2)}) collective-permute-start(bf16[4,16384]{1,0:T(4,128)(2,1)S(1)} %collective-permute-done), channel_id=1, source_target_pairs={{0,4},{4,8},{8,12},{12,0},{1,5},{5,9},{9,13},{13,1},{2,6},{6,10},{... | collective-permute-start | bytes 393224 | tf_op jit(solution)/shard_map/ppermute | solution.py:17
  24.2 21.7 %copy-start = (u32[32]{0:T(128)S(1)}, u32[32]{0:T(128)}, u32[]{:S(2)}) copy-start(u32[32]{0:T(128)} %constant.58) | copy-start | bytes 388
  45.8 112.5 %all-reduce.7.cloned.1.call-start = ((), (), s32[]{:S(2)}) async-start(), calls=%async_computation.1 | async-start | bytes 1048576
  85.0 7.7 %collective-permute-start.3 = (bf16[4,16384]{1,0:T(4,128)(2,1)S(1)}, bf16[4,16384]{1,0:T(4,128)(2,1)S(1)}, u32[]{:S(2)}, u32[]{:S(2)}) collective-permute-start(bf16[4,16384]{1,0:T(4,128)(2,1)S(1)} %get-tuple-element.8), channel_id=1, source_target_pairs={{0,4},{4,8},{8,12},{12,0},{1,5},{5,9},{9,13},{13,1},{2,6},{6,10},{... | collective-permute-start | bytes 393224 | tf_op jit(solution)/shard_map/ppermute | solution.py:17
  86.3 7.0 %collective-permute-start.4 = (bf16[4,16384]{1,0:T(4,128)(2,1)S(1)}, bf16[4,16384]{1,0:T(4,128)(2,1)S(1)}, u32[]{:S(2)}, u32[]{:S(2)}) collective-permute-start(bf16[4,16384]{1,0:T(4,128)(2,1)S(1)} %get-tuple-element.8), channel_id=1, source_target_pairs={{0,12},{4,0},{8,4},{12,8},{1,13},{5,1},{9,5},{13,9},{2,14},{6,2},{... | collective-permute-start | bytes 393224 | tf_op jit(solution)/shard_map/ppermute | solution.py:20
  92.7 6.8 %collective-permute-start.5 = (bf16[4,16384]{1,0:T(4,128)(2,1)S(1)}, bf16[4,16384]{1,0:T(4,128)(2,1)S(1)}, u32[]{:S(2)}, u32[]{:S(2)}) collective-permute-start(bf16[4,16384]{1,0:T(4,128)(2,1)S(1)} %collective-permute-done.3), channel_id=1, source_target_pairs={{0,4},{4,8},{8,12},{12,0},{1,5},{5,9},{9,13},{13,1},{2,6},{6,10},{... | collective-permute-start | bytes 393224 | tf_op jit(solution)/shard_map/ppermute | solution.py:17
Sparse Core Ops, SparseCore 0:
  45.9 37.8 all-reduce.4
  121.5 36.7 all-reduce.6
